TPU v7x, 32 devices: a whole 2x2x4 slice. The times are simulated.
32 devices in a mesh: col: 8 (over y, x, core), dev: 4 (over z).
Axes of the slice: x: 2, y: 2, z: 4, core: 2. Of those that a mesh axis runs over, the one named last changes fastest.
Arguments:
- first_factor: bfloat16 [16, 1024, 2048], P(None, 'col', 'dev'), may hold values from -1 to 1
- second_factor: bfloat16 [16, 1024, 2048], P(None, 'dev', 'col'), may hold values from -1 to 1
- amplitudes: bfloat16 [512, 1024, 1024], P(None, 'col', 'dev'), may hold values from -0.0059814453 to 0.0059814453
Outputs:
- ladder: float32 [512, 256], P(('col', 'dev'))
All inputs are finite; a program needn't handle non-finite values.
Results may differ from a plain program's by a relative error of at most 0.0029.
Values may be sent and summed in bfloat16 or wider, within the bound.
A program may use at most 128 MiB of HBM per device.

v0:
```python
import jax
import jax.numpy as jnp
from jax import lax
from jax.sharding import PartitionSpec as P


def on_device(first_factor, second_factor, amplitudes):
    width_a, block_c, _ = first_factor.shape
    width_b, block_d, _ = second_factor.shape
    pairs = amplitudes.shape[0]
    first_whole = lax.all_gather(first_factor, "dev", axis=2, tiled=True).reshape(
        width_a * block_c, -1
    )
    second_whole = lax.all_gather(second_factor, "col", axis=2, tiled=True).reshape(
        width_b * block_d, -1
    )
    tile_sum = lax.dot_general(
        first_whole, second_whole, (((1,), (1,)), ((), ())), preferred_element_type=jnp.float32
    )
    tile = tile_sum.astype(jnp.bfloat16).reshape(width_a, block_c, width_b, block_d)
    partial_value = jnp.einsum(
        "acbd,pcd->pab", tile, amplitudes, preferred_element_type=jnp.float32
    )
    partial_value = partial_value.reshape(pairs, width_a * width_b)
    halfway = lax.psum_scatter(partial_value, "col", scatter_dimension=0, tiled=True)
    return lax.psum_scatter(halfway, "dev", scatter_dimension=0, tiled=True)


def solution(mesh):
    placed = (P(None, "col", "dev"), P(None, "dev", "col"), P(None, "col", "dev"))
    return jax.shard_map(
        on_device, mesh=mesh, in_specs=placed, out_specs=P(("col", "dev"), None), check_vma=False
    )
```

profile of v0, /device:TPU:0, one launch (start us, length us, event | category | flops | bytes accessed | tf_op | source)
XLA Modules:
  0.0 409.0 jit_solution(3210589852640393744)
XLA Ops:
  6.5 0.0 all-gather.3.cloned.1.call-start
  6.5 0.7 all-gather.3.cloned.1.call-update
  7.3 0.0 all-gather.5.cloned.1.call-start
  7.3 0.7 all-gather.5.cloned.1.call-update
  8.0 0.0 reduce-scatter.3.cloned.1.call-start
  8.1 153.2 %all-gather.3.cloned.1.call-done = bf16[16,128,2048]{2,1,0:T(8,128)(2,1)} async-done(((bf16[16,128,512]{2,1,0:T(8,128)(2,1)}), bf16[16,128,2048]{2,1,0:T(8,128)(2,1)}) %all-gather.3.cloned.1.call-update) | async-done | bytes 8388624 | tf_op jit(solution)/shard_map/all_gather | solution.py:11
  161.3 93.1 %all-gather.5.cloned.1.call-done = bf16[16,256,2048]{2,1,0:T(8,128)(2,1)} async-done(((bf16[16,256,256]{2,1,0:T(8,128)(2,1)}), bf16[16,256,2048]{2,1,0:T(8,128)(2,1)}) %all-gather.5.cloned.1.call-update) | async-done | bytes 16777232 | tf_op jit(solution)/shard_map/all_gather | solution.py:14
  254.4 40.6 %convolution_convert_fusion = bf16[2048,4096]{1,0:T(8,128)(2,1)S(1)} fusion(bf16[2048,2048]{1,0:T(8,128)(2,1)} %bitcast.24, bf16[4096,2048]{1,0:T(8,128)(2,1)} %bitcast.23), kind=kOutput, calls=%fused_computation.4 | convolution fusion | flops 34368126976 | bytes 41943040 | tf_op jit(solution)/shard_map/dot_general | solution.py:17
  295.0 8.7 %copy.7 = bf16[256,8,16,256]{3,2,1,0:T(8,128)(2,1)} copy(bf16[256,8,16,256]{3,1,2,0:T(8,128)(2,1)S(1)} %bitcast.20) | data formatting | bytes 33554432
  303.8 42.0 %fusion = f32[16,16,512,1]{2,1,3,0:T(8,128)S(1)} fusion(bf16[512,128,256]{2,1,0:T(8,128)(2,1)} %param.5, bf16[16,128,16,256]{3,2,1,0:T(8,128)(2,1)} %bitcast.21), kind=kOutput, calls=%fused_computation | convolution fusion | flops 8589934592 | bytes 50855936 | tf_op jit(solution)/shard_map/acbd,pcd->pab/dot_general | solution.py:21
  345.7 1.0 copy.5
  346.7 0.0 reduce-scatter.3.cloned.1.call-update
  346.8 0.0 reduce-scatter.5.cloned.1.call-start
  346.8 34.2 %reduce-scatter.3.cloned.1.call-done = f32[64,256]{1,0:T(8,128)} async-done(((f32[512,256]{1,0:T(8,128)}), f32[64,256]{1,0:T(8,128)}) %reduce-scatter.3.cloned.1.call-update) | async-done | bytes 65552 | tf_op jit(solution)/shard_map/reduce_scatter | solution.py:25
  381.0 0.0 reduce-scatter.5.cloned.1.call-update
  381.1 21.4 %reduce-scatter.5.cloned.1.call-done = f32[16,256]{1,0:T(8,128)} async-done(((f32[64,256]{1,0:T(8,128)}), f32[16,256]{1,0:T(8,128)}) %reduce-scatter.5.cloned.1.call-update) | async-done | bytes 16400 | tf_op jit(solution)/shard_map/reduce_scatter | solution.py:26
Async XLA Ops:
  6.5 154.7 %all-gather.3.cloned.1.call-start = ((), (), s32[]{:S(2)}) async-start(), calls=%async_computation.2 | async-start | bytes 10485760 | tf_op jit(solution)/shard_map/all_gather | solution.py:11
  7.3 247.1 %all-gather.5.cloned.1.call-start = ((), (), s32[]{:S(2)}) async-start(), calls=%async_computation.3 | async-start | bytes 18874368 | tf_op jit(solution)/shard_map/all_gather | solution.py:14
  8.0 373.0 %reduce-scatter.3.cloned.1.call-start = ((), (), s32[]{:S(2)}) async-start(), calls=%async_computation.4 | async-start | bytes 589824 | tf_op jit(solution)/shard_map/reduce_scatter | solution.py:25
  346.8 55.7 %reduce-scatter.5.cloned.1.call-start = ((), (), s32[]{:S(2)}) async-start(), calls=%async_computation.5 | async-start | bytes 81920 | tf_op jit(solution)/shard_map/reduce_scatter | solution.py:26
Sparse Core Ops, SparseCore 0:
  8.9 152.3 all-gather.2
  163.1 91.1 all-gather.4
  346.9 34.1 reduce-scatter.2
  383.1 19.2 reduce-scatter.4
where the time goes:
time: 409 us
  waiting for transfers between devices  303 us (74%)
  matrix products  82.6 us (20%)
  between operations  13.1 us (3%)
  local copies, waits for them, and re-layouts  9.73 us (2%)
    all_gather x1, waiting for transfers between devices, on_device(): lax.all_gather(first_factor, 'dev', axis=2, tiled=True)  153 us
    all_gather x1, waiting for transfers between devices, on_device(): lax.all_gather(second_factor, 'col', axis=2, tiled=True)  93.1 us
    dot_general x1, matrix products, on_device(): jnp.einsum('acbd,pcd->pab', tile, amplitudes, preferred_element_type=jnp....  42 us
    dot_general x1, matrix products, on_device(): lax.dot_general(first_whole, second_whole, (((1,), (1,)), ((), ())), pref...  40.6 us
    reduce_scatter x1, waiting for transfers between devices, on_device(): lax.psum_scatter(partial_value, 'col', scatter_dimension=0, tiled=True)  34.2 us
    reduce_scatter x1, waiting for transfers between devices, on_device(): return lax.psum_scatter(halfway, 'dev', scatter_dimension=0, tiled=True)  21.4 us
    unnamed x1, local copies, waits for them, and re-layouts  8.73 us
  transfers between devices with their start and end apart: 4, of which 4 were waited for; matrix products, arithmetic and copies ran while one was open for 0% of the time, Pallas kernels for 0%

commit v1 on v0

--- a/solution.py
+++ b/solution.py
@@ -2,6 +2,17 @@
 import jax.numpy as jnp
 from jax import lax
 from jax.sharding import PartitionSpec as P
+
+
+def ring_gather(value, axis, dim):
+    ways = lax.axis_size(axis)
+    pieces = [value]
+    for far in range(1, ways):
+        pieces.append(
+            lax.ppermute(pieces[far - 1], axis, [(d, (d - 1) % ways) for d in range(ways)])
+        )
+    line = jnp.concatenate(pieces, axis=dim)
+    return jnp.roll(line, lax.axis_index(axis) * value.shape[dim], axis=dim)
 
 
 def on_device(first_factor, second_factor, amplitudes):
@@ -11,9 +22,7 @@
     first_whole = lax.all_gather(first_factor, "dev", axis=2, tiled=True).reshape(
         width_a * block_c, -1
     )
-    second_whole = lax.all_gather(second_factor, "col", axis=2, tiled=True).reshape(
-        width_b * block_d, -1
-    )
+    second_whole = ring_gather(second_factor, "col", 2).reshape(width_b * block_d, -1)
     tile_sum = lax.dot_general(
         first_whole, second_whole, (((1,), (1,)), ((), ())), preferred_element_type=jnp.float32
     )

time: 409 us -> 393 us (0.961)
  waiting for transfers between devices: 303 us -> 197 us
  local copies, waits for them, and re-layouts: 9.73 us -> 94.5 us
  starting transfers between devices: 0.12 us -> 21.7 us
  matrix products: 82.6 us -> 64.5 us
    all_gather x1, waiting for transfers between devices: 153 us -> 0.01 us  [on_device(): lax.all_gather(first_factor, 'dev', axis=2, tiled=True)]
    ppermute x0 -> x7, waiting for transfers between devices: none -> 142 us  [ring_gather(): lax.ppermute(pieces[far - 1], axis, [(d, (d - 1) % ways) for d in range(w...]
    all_gather x1 -> x0, waiting for transfers between devices: 93.1 us -> none  [on_device(): lax.all_gather(second_factor, 'col', axis=2, tiled=True)]
    unnamed x1 -> x33, local copies, waits for them, and re-layouts: 8.73 us -> 84.7 us
    ppermute x0 -> x7, starting transfers between devices: none -> 21.6 us  [ring_gather(): lax.ppermute(pieces[far - 1], axis, [(d, (d - 1) % ways) for d in range(w...]
    dot_general x1, matrix products: 42 us -> 22.5 us  [on_device(): jnp.einsum('acbd,pcd->pab', tile, amplitudes, preferred_element_type=jnp....]
    dynamic_slice x0 -> x1, local copies, waits for them, and re-layouts: none -> 6.63 us  [ring_gather(): return jnp.roll(line, lax.axis_index(axis) * value.shape[dim], axis=dim)]
  transfers between devices with their start and end apart: 4 -> 10, of which waited for: 4 -> 8; matrix products, arithmetic and copies ran while one was open for 0% -> 20% of each run, Pallas kernels for 0% -> 0%
where the time goes in v1:
time: 393 us; the launch traced here: 391 us
  waiting for transfers between devices  197 us (50%)
  local copies, waits for them, and re-layouts  94.5 us (24%)
  matrix products  64.5 us (16%)
  starting transfers between devices  21.7 us (6%)
  between operations  13.3 us (3%)
    ppermute x7, waiting for transfers between devices, ring_gather(): lax.ppermute(pieces[far - 1], axis, [(d, (d - 1) % ways) for d in range(w...  142 us
    unnamed x33, local copies, waits for them, and re-layouts  84.7 us
    dot_general x1, matrix products, on_device(): lax.dot_general(first_whole, second_whole, (((1,), (1,)), ((), ())), pref...  42 us
    reduce_scatter x1, waiting for transfers between devices, on_device(): lax.psum_scatter(partial_value, 'col', scatter_dimension=0, tiled=True)  33.6 us
    dot_general x1, matrix products, on_device(): jnp.einsum('acbd,pcd->pab', tile, amplitudes, preferred_element_type=jnp....  22.5 us
    ppermute x7, starting transfers between devices, ring_gather(): lax.ppermute(pieces[far - 1], axis, [(d, (d - 1) % ways) for d in range(w...  21.6 us
    reduce_scatter x1, waiting for transfers between devices, on_device(): return lax.psum_scatter(halfway, 'dev', scatter_dimension=0, tiled=True)  21.6 us
  transfers between devices with their start and end apart: 10, of which 8 were waited for; matrix products, arithmetic and copies ran while one was open for 20% of the time, Pallas kernels for 0%

profile of v1, /device:TPU:0, one launch (start us, length us, event | category | flops | bytes accessed | tf_op | source)
XLA Modules:
  0.0 391.1 jit_solution(609703380871732549)
XLA Ops:
  6.5 0.0 all-gather.2.cloned.1.call-start
  6.5 3.4 collective-permute-start
  9.9 23.9 %collective-permute-done = bf16[16,256,256]{2,1,0:T(8,128)(2,1)S(1)} collective-permute-done((bf16[16,256,256]{2,1,0:T(8,128)(2,1)}, bf16[16,256,256]{2,1,0:T(8,128)(2,1)S(1)}, u32[]{:S(2)}, u32[]{:S(2)}) %collective-permute-start) | collective-permute-done | bytes 2097184 | tf_op jit(solution)/shard_map/ppermute | solution.py:12
  33.8 0.0 copy-start.1
  33.8 1.3 copy-done.1
  35.1 2.7 collective-permute-start.1
  37.8 23.6 %collective-permute-done.1 = bf16[16,256,256]{2,1,0:T(8,128)(2,1)S(1)} collective-permute-done((bf16[16,256,256]{2,1,0:T(8,128)(2,1)S(1)}, bf16[16,256,256]{2,1,0:T(8,128)(2,1)S(1)}, u32[]{:S(2)}, u32[]{:S(2)}) %collective-permute-start.1) | collective-permute-done | bytes 2097184 | tf_op jit(solution)/shard_map/ppermute | solution.py:12
  61.3 0.0 copy-start.3
  61.3 2.8 collective-permute-start.2
  64.1 0.0 all-gather.2.cloned.1.call-update
  64.2 0.0 reduce-scatter.3.cloned.1.call-start
  64.2 23.5 %collective-permute-done.2 = bf16[16,256,256]{2,1,0:T(8,128)(2,1)} collective-permute-done((bf16[16,256,256]{2,1,0:T(8,128)(2,1)S(1)}, bf16[16,256,256]{2,1,0:T(8,128)(2,1)}, u32[]{:S(2)}, u32[]{:S(2)}) %collective-permute-start.2) | collective-permute-done | bytes 2097184 | tf_op jit(solution)/shard_map/ppermute | solution.py:12
  87.7 3.2 collective-permute-start.3
  90.9 23.9 %collective-permute-done.3 = bf16[16,256,256]{2,1,0:T(8,128)(2,1)S(1)} collective-permute-done((bf16[16,256,256]{2,1,0:T(8,128)(2,1)}, bf16[16,256,256]{2,1,0:T(8,128)(2,1)S(1)}, u32[]{:S(2)}, u32[]{:S(2)}) %collective-permute-start.3) | collective-permute-done | bytes 2097184 | tf_op jit(solution)/shard_map/ppermute | solution.py:12
  114.8 0.0 copy-start.5
  114.8 1.3 copy-done.5
  116.1 3.1 collective-permute-start.4
  119.2 23.6 %collective-permute-done.4 = bf16[16,256,256]{2,1,0:T(8,128)(2,1)S(1)} collective-permute-done((bf16[16,256,256]{2,1,0:T(8,128)(2,1)S(1)}, bf16[16,256,256]{2,1,0:T(8,128)(2,1)S(1)}, u32[]{:S(2)}, u32[]{:S(2)}) %collective-permute-start.4) | collective-permute-done | bytes 2097184 | tf_op jit(solution)/shard_map/ppermute | solution.py:12
  142.8 0.0 copy-start.7
  142.8 1.4 copy-done.7
  144.1 3.2 collective-permute-start.5
  147.3 23.6 %collective-permute-done.5 = bf16[16,256,256]{2,1,0:T(8,128)(2,1)} collective-permute-done((bf16[16,256,256]{2,1,0:T(8,128)(2,1)S(1)}, bf16[16,256,256]{2,1,0:T(8,128)(2,1)}, u32[]{:S(2)}, u32[]{:S(2)}) %collective-permute-start.5) | collective-permute-done | bytes 2097184 | tf_op jit(solution)/shard_map/ppermute | solution.py:12
  170.9 3.2 collective-permute-start.6
  174.1 0.0 copy-done.3
  174.1 0.0 copy-start
  174.1 50.4 %copy.8 = bf16[512,128,256,1]{0,1,2,3:T(8,128)(2,1)} copy(bf16[512,128,256,1]{2,1,0,3:T(8,128)(2,1)} %bitcast.19) | data formatting | bytes 67108864 | tf_op args[2]
  224.5 0.0 copy-done
  224.5 0.0 copy-start.2
  224.5 0.0 copy-start.4
  224.5 0.0 copy-start.6
  224.6 0.3 constant_dynamic-update-slice_fusion.15
  224.8 2.0 constant_dynamic-update-slice_fusion.14
  226.9 2.0 constant_dynamic-update-slice_fusion.13
  228.9 1.9 constant_dynamic-update-slice_fusion.12
  230.8 1.9 constant_dynamic-update-slice_fusion.11
  232.7 1.9 constant_dynamic-update-slice_fusion.10
  234.6 1.9 constant_dynamic-update-slice_fusion.9
  236.5 0.0 collective-permute-done.6
  236.5 1.9 constant_dynamic-update-slice_fusion.8
  238.4 0.3 constant_dynamic-update-slice_fusion.7
  238.7 0.0 copy-done.2
  238.7 0.3 constant_dynamic-update-slice_fusion.6
  239.0 0.0 copy-done.4
  239.0 0.3 constant_dynamic-update-slice_fusion.5
  239.3 1.9 constant_dynamic-update-slice_fusion.4
  241.2 0.0 copy-done.6
  241.2 0.3 constant_dynamic-update-slice_fusion.3
  241.5 1.9 constant_dynamic-update-slice_fusion.2
  243.4 1.9 constant_dynamic-update-slice_fusion.1
  245.3 1.9 constant_dynamic-update-slice_fusion
  247.2 6.6 %constant_dynamic-slice_fusion = bf16[16,256,2048]{2,1,0:T(8,128)(2,1)} fusion(bf16[16,256,4096]{2,1,0:T(8,128)(2,1)S(1)} %constant_dynamic-update-slice_fusion, s32[]{:T(128)S(6)} %select_n.14), kind=kLoop, calls=%fused_computation.17 | loop fusion | bytes 33554436 | tf_op jit(solution)/shard_map/jit(_roll_dynamic)/dynamic_slice | solution.py:15
  253.8 0.0 all-gather.2.cloned.1.call-done
  253.8 42.0 %convert_bitcast_fusion = bf16[512,8,16,128]{3,1,2,0:T(8,128)(2,1)} fusion(bf16[4096,2048]{1,0:T(8,128)(2,1)} %bitcast.20, bf16[2048,2048]{1,0:T(8,128)(2,1)} %bitcast.23), kind=kOutput, calls=%fused_computation | convolution fusion | flops 34368126976 | bytes 41943040 | tf_op jit(solution)/shard_map/dot_general | solution.py:26
  295.8 9.6 %copy.12 = bf16[512,8,16,128]{3,2,1,0:T(8,128)(2,1)S(1)} copy(bf16[512,8,16,128]{3,1,2,0:T(8,128)(2,1)} %convert_bitcast_fusion) | data formatting | bytes 33554432
  305.5 22.5 %fusion = f32[16,16,512,1]{2,0,3,1:T(8,128)S(1)} fusion(bf16[16,128,16,256]{1,0,3,2:T(8,128)(2,1)S(1)} %bitcast.21, bf16[512,128,256,1]{0,1,2,3:T(8,128)(2,1)} %copy.8), kind=kOutput, calls=%fused_computation.18 | convolution fusion | flops 8589934592 | bytes 50855936 | tf_op jit(solution)/shard_map/acbd,pcd->pab/dot_general | solution.py:30
  328.0 0.3 copy.9
  328.3 1.0 copy.6
  329.3 0.0 reduce-scatter.3.cloned.1.call-update
  329.3 0.0 reduce-scatter.5.cloned.1.call-start
  329.4 33.6 %reduce-scatter.3.cloned.1.call-done = f32[64,256]{1,0:T(8,128)} async-done(((f32[512,256]{1,0:T(8,128)}), f32[64,256]{1,0:T(8,128)}) %reduce-scatter.3.cloned.1.call-update) | async-done | bytes 65552 | tf_op jit(solution)/shard_map/reduce_scatter | solution.py:34
  363.0 0.0 reduce-scatter.5.cloned.1.call-update
  363.0 21.6 %reduce-scatter.5.cloned.1.call-done = f32[16,256]{1,0:T(8,128)} async-done(((f32[64,256]{1,0:T(8,128)}), f32[16,256]{1,0:T(8,128)}) %reduce-scatter.5.cloned.1.call-update) | async-done | bytes 16400 | tf_op jit(solution)/shard_map/reduce_scatter | solution.py:35
Async XLA Ops:
  6.5 247.3 %all-gather.2.cloned.1.call-start = ((), (), s32[]{:S(2)}) async-start(), calls=%async_computation.2 | async-start | bytes 10485760 | tf_op jit(solution)/shard_map/all_gather | solution.py:22
  6.5 27.2 %collective-permute-start = (bf16[16,256,256]{2,1,0:T(8,128)(2,1)}, bf16[16,256,256]{2,1,0:T(8,128)(2,1)S(1)}, u32[]{:S(2)}, u32[]{:S(2)}) collective-permute-start(bf16[16,256,256]{2,1,0:T(8,128)(2,1)} %param.4), channel_id=1, source_target_pairs={{0,28},{4,0},{8,4},{12,8},{16,12},{20,16},{24,20},{28,24},{1,29},{... | collective-permute-start | bytes 6291464 | tf_op jit(solution)/shard_map/ppermute | solution.py:12
  33.8 1.3 copy-start.1
  35.1 26.3 %collective-permute-start.1 = (bf16[16,256,256]{2,1,0:T(8,128)(2,1)S(1)}, bf16[16,256,256]{2,1,0:T(8,128)(2,1)S(1)}, u32[]{:S(2)}, u32[]{:S(2)}) collective-permute-start(bf16[16,256,256]{2,1,0:T(8,128)(2,1)S(1)} %collective-permute-done), channel_id=1, source_target_pairs={{0,28},{4,0},{8,4},{12,8},{16,12},{20,16},{24,20},{28,24},{1,29},{... | collective-permute-start | bytes 6291464 | tf_op jit(solution)/shard_map/ppermute | solution.py:12
  61.3 112.8 %copy-start.3 = (bf16[16,256,256]{2,1,0:T(8,128)(2,1)}, bf16[16,256,256]{2,1,0:T(8,128)(2,1)S(1)}, u32[]{:S(2)}) copy-start(bf16[16,256,256]{2,1,0:T(8,128)(2,1)S(1)} %collective-permute-done.1) | copy-start | bytes 6291460
  61.3 26.4 %collective-permute-start.2 = (bf16[16,256,256]{2,1,0:T(8,128)(2,1)S(1)}, bf16[16,256,256]{2,1,0:T(8,128)(2,1)}, u32[]{:S(2)}, u32[]{:S(2)}) collective-permute-start(bf16[16,256,256]{2,1,0:T(8,128)(2,1)S(1)} %collective-permute-done.1), channel_id=1, source_target_pairs={{0,28},{4,0},{8,4},{12,8},{16,12},{20,16},{24,20},{28,24},{1,29},{... | collective-permute-start | bytes 6291464 | tf_op jit(solution)/shard_map/ppermute | solution.py:12
  64.2 298.8 %reduce-scatter.3.cloned.1.call-start = ((), (), s32[]{:S(2)}) async-start(), calls=%async_computation.3 | async-start | bytes 589824 | tf_op jit(solution)/shard_map/reduce_scatter | solution.py:34
  87.7 27.1 %collective-permute-start.3 = (bf16[16,256,256]{2,1,0:T(8,128)(2,1)}, bf16[16,256,256]{2,1,0:T(8,128)(2,1)S(1)}, u32[]{:S(2)}, u32[]{:S(2)}) collective-permute-start(bf16[16,256,256]{2,1,0:T(8,128)(2,1)} %collective-permute-done.2), channel_id=1, source_target_pairs={{0,28},{4,0},{8,4},{12,8},{16,12},{20,16},{24,20},{28,24},{1,29},{... | collective-permute-start | bytes 6291464 | tf_op jit(solution)/shard_map/ppermute | solution.py:12
  114.8 1.3 copy-start.5
  116.1 26.7 %collective-permute-start.4 = (bf16[16,256,256]{2,1,0:T(8,128)(2,1)S(1)}, bf16[16,256,256]{2,1,0:T(8,128)(2,1)S(1)}, u32[]{:S(2)}, u32[]{:S(2)}) collective-permute-start(bf16[16,256,256]{2,1,0:T(8,128)(2,1)S(1)} %collective-permute-done.3), channel_id=1, source_target_pairs={{0,28},{4,0},{8,4},{12,8},{16,12},{20,16},{24,20},{28,24},{1,29},{... | collective-permute-start | bytes 6291464 | tf_op jit(solution)/shard_map/ppermute | solution.py:12
  142.8 1.4 copy-start.7
  144.1 26.8 %collective-permute-start.5 = (bf16[16,256,256]{2,1,0:T(8,128)(2,1)S(1)}, bf16[16,256,256]{2,1,0:T(8,128)(2,1)}, u32[]{:S(2)}, u32[]{:S(2)}) collective-permute-start(bf16[16,256,256]{2,1,0:T(8,128)(2,1)S(1)} %collective-permute-done.4), channel_id=1, source_target_pairs={{0,28},{4,0},{8,4},{12,8},{16,12},{20,16},{24,20},{28,24},{1,29},{... | collective-permute-start | bytes 6291464 | tf_op jit(solution)/shard_map/ppermute | solution.py:12
  170.9 65.6 %collective-permute-start.6 = (bf16[16,256,256]{2,1,0:T(8,128)(2,1)}, bf16[16,256,256]{2,1,0:T(8,128)(2,1)}, u32[]{:S(2)}, u32[]{:S(2)}) collective-permute-start(bf16[16,256,256]{2,1,0:T(8,128)(2,1)} %collective-permute-done.5), channel_id=1, source_target_pairs={{0,28},{4,0},{8,4},{12,8},{16,12},{20,16},{24,20},{28,24},{1,29},{... | collective-permute-start | bytes 6291464 | tf_op jit(solution)/shard_map/ppermute | solution.py:12
  174.1 50.4 %copy-start = (bf16[16,256,256]{2,1,0:T(8,128)(2,1)S(1)}, bf16[16,256,256]{2,1,0:T(8,128)(2,1)}, u32[]{:S(2)}) copy-start(bf16[16,256,256]{2,1,0:T(8,128)(2,1)} %param.4) | copy-start | bytes 6291460
  224.5 14.1 %copy-start.2 = (bf16[16,256,256]{2,1,0:T(8,128)(2,1)S(1)}, bf16[16,256,256]{2,1,0:T(8,128)(2,1)}, u32[]{:S(2)}) copy-start(bf16[16,256,256]{2,1,0:T(8,128)(2,1)} %copy-done.1) | copy-start | bytes 6291460
  224.5 14.5 %copy-start.4 = (bf16[16,256,256]{2,1,0:T(8,128)(2,1)S(1)}, bf16[16,256,256]{2,1,0:T(8,128)(2,1)}, u32[]{:S(2)}) copy-start(bf16[16,256,256]{2,1,0:T(8,128)(2,1)} %copy-done.3) | copy-start | bytes 6291460
  224.5 16.7 %copy-start.6 = (bf16[16,256,256]{2,1,0:T(8,128)(2,1)S(1)}, bf16[16,256,256]{2,1,0:T(8,128)(2,1)}, u32[]{:S(2)}) copy-start(bf16[16,256,256]{2,1,0:T(8,128)(2,1)} %copy-done.5) | copy-start | bytes 6291460
  329.3 55.2 %reduce-scatter.5.cloned.1.call-start = ((), (), s32[]{:S(2)}) async-start(), calls=%async_computation.4 | async-start | bytes 81920 | tf_op jit(solution)/shard_map/reduce_scatter | solution.py:35
Sparse Core Ops, SparseCore 0:
  64.3 148.9 all-gather.1
  329.4 33.5 reduce-scatter.2
  365.2 19.2 reduce-scatter.4
